TPU v7x, 32 devices: a whole 2x2x4 slice. The times are simulated.
32 devices in a mesh: range: 16 (over z, y, x), chip: 2 (over core).
Axes of the slice: x: 2, y: 2, z: 4, core: 2. Of those that a mesh axis runs over, the one named last changes fastest.
Arguments:
- mode_tables: bfloat16 [32, 2048, 768], P('range', None, 'chip'), may hold values from -1 to 1
- attenuation: float32 [32, 768], P('range'), may hold values from 0 to 1, as said below
- excitation: float32 [768, 128], replicated, may hold values from -6 to 6
Outputs:
- fields: float32 [32, 2048, 128], P('range', 'chip')
Inputs may be any that keep to these rules, and one draw needn't show every extreme that they name: attenuation rates, positive.
All inputs are finite; a program needn't handle non-finite values.
Results may differ from a plain program's by a relative error of at most 0.0029.
Values may be sent and summed in bfloat16 or wider, within the bound.
A program may use at most 64 MiB of HBM per device.

v0:
```python
import jax
import jax.numpy as jnp
from jax import lax
from jax.sharding import PartitionSpec as P

highest = lax.Precision.HIGHEST


def from_behind(value, axis, steps):
    count = lax.axis_size(axis)
    initial, last = (max(0, -steps), min(count, count - steps))
    return lax.ppermute(value, axis, [(source, source + steps) for source in range(initial, last)])


def on_device(mode_tables, attenuation, excitation):
    seg_local, height_count, half_count = mode_tables.shape
    chip_count = lax.axis_size("chip")
    count_of_modes = half_count * chip_count
    range_count = lax.axis_size("range")
    position = lax.axis_index("range")
    core_index = lax.axis_index("chip")
    is_first = position == 0
    column_start = core_index * half_count
    identity = jnp.eye(count_of_modes, dtype=jnp.float32)
    damping = jnp.exp(-attenuation)
    earlier_half = from_behind(mode_tables[seg_local - 1], "range", 1)
    tables, earlier = (
        lax.all_gather(mode_tables, "chip", axis=2, tiled=True),
        lax.all_gather(earlier_half, "chip", axis=1, tiled=True),
    )
    previous = jnp.concatenate([earlier[None], tables[:-1]], axis=0)
    intersection = jnp.einsum("shm,shn->smn", tables, previous, preferred_element_type=jnp.float32)
    intersection = intersection.at[0].set(jnp.where(is_first, identity, intersection[0]))
    matrices = damping[:, :, None] * intersection
    prefix = lax.dynamic_slice_in_dim(matrices[0], column_start, half_count, 1)
    segment = 1
    prefix = jnp.dot(matrices[segment], prefix, precision=highest)
    rounds = (range_count - 1).bit_length()
    for level_index in range(rounds):
        distance = 2**level_index
        earlier_part = from_behind(prefix, "range", distance)
        product = jnp.dot(
            lax.all_gather(prefix, "chip", axis=1, tiled=True), earlier_part, precision=highest
        )
        prefix = jnp.where(position >= distance, product, prefix)
    source_rows = lax.dynamic_slice_in_dim(excitation, column_start, half_count, 0)
    reached = lax.psum(jnp.dot(prefix, source_rows, precision=highest), "chip")
    arriving = from_behind(reached, "range", 1)
    amplitude = jnp.where(is_first, excitation, arriving)
    stored = []
    segment = 0
    amplitude = jnp.dot(matrices[segment], amplitude, precision=highest)
    stored.append(amplitude.astype(jnp.bfloat16))
    stored.append(reached.astype(jnp.bfloat16))
    rounded = jnp.stack(stored)
    row_count = height_count // chip_count
    own_rows = lax.dynamic_slice_in_dim(tables, core_index * row_count, row_count, 1)
    return jnp.einsum("shm,smc->shc", own_rows, rounded, preferred_element_type=jnp.float32)


def solution(mesh):
    placed = (P("range", None, "chip"), P("range", None), P())
    return jax.shard_map(
        on_device, mesh=mesh, in_specs=placed, out_specs=P("range", "chip", None), check_vma=False
    )
```

profile of v0, /device:TPU:31, one launch (start us, length us, event | category | flops | bytes accessed | tf_op | source)
XLA Modules:
  0.0 301.9 jit_solution(1678558240698443344)
XLA Ops:
  8.6 1.3 collective-permute-start
  9.9 35.9 %collective-permute-done = bf16[2048,384]{1,0:T(8,128)(2,1)S(1)} collective-permute-done((bf16[2048,384]{1,0:T(8,128)(2,1)S(1)}, bf16[2048,384]{1,0:T(8,128)(2,1)S(1)}, u32[]{:S(2)}, u32[]{:S(2)}) %collective-permute-start) | collective-permute-done | bytes 1572896 | tf_op jit(solution)/shard_map/ppermute | solution.py:12
  47.1 14.5 %all-gather.9.cloned.1.call-done = bf16[2048,768]{1,0:T(8,128)(2,1)} async-done(((bf16[2048,384]{1,0:T(8,128)(2,1)}), bf16[2048,768]{1,0:T(8,128)(2,1)}) %all-gather.9.cloned.1.call-update) | async-done | bytes 3145744 | tf_op jit(solution)/shard_map/all_gather | solution.py:29
  61.6 9.8 %fusion.10 = f32[2,768,768]{1,2,0:T(8,128)S(1)} fusion(bf16[2,2048,768]{2,1,0:T(8,128)(2,1)} %all-gather.7.cloned.1.call-done, bf16[1,2048,768]{2,1,0:T(8,128)(2,1)S(1)} %slice-done, bf16[1,2048,768]{2,1,0:T(8,128)(2,1)} %bitcast.32), kind=kOutput, calls=%fused_computation.14 | convolution fusion | flops 4834983936 | bytes 17301504 | tf_op jit(solution)/shard_map/shm,shn->smn/dot_general | solution.py:32
  72.3 2.1 copy-done
  74.4 8.7 %fusion.6 = f32[768,384]{1,0:T(8,128)} fusion(f32[2,768,768]{1,2,0:T(8,128)S(1)} %broadcast_multiply_fusion, f32[1,768,768]{1,2,0:T(8,128)S(1)} %slice.43, s32[]{:T(128)S(6)} %select_n.58), kind=kOutput, calls=%fused_computation.7 | convolution fusion | flops 2717908992 | bytes 4718596 | tf_op jit(solution)/shard_map/dot_general | solution.py:37
  83.2 1.3 collective-permute-start.1
  84.5 28.1 %collective-permute-done.1 = f32[768,384]{1,0:T(8,128)S(1)} collective-permute-done((f32[768,384]{1,0:T(8,128)}, f32[768,384]{1,0:T(8,128)S(1)}, u32[]{:S(2)}, u32[]{:S(2)}) %collective-permute-start.1) | collective-permute-done | bytes 1179680 | tf_op jit(solution)/shard_map/ppermute | solution.py:12
  112.6 6.5 %convolution_select_fusion.3 = f32[768,384]{1,0:T(8,128)} fusion(f32[768,384]{1,0:T(8,128)} %fusion.6, f32[768,768]{1,0:T(8,128)} %all-gather.11.cloned.1.call-done, f32[768,384]{1,0:T(8,128)S(1)} %collective-permute-done.1, pred[]{:T(512)S(6)} %ge.15), kind=kOutput, calls=%fused_computation.19 | convolution fusion | flops 2718203904 | bytes 5898241 | tf_op jit(solution)/shard_map/dot_general | solution.py:42
  119.2 1.3 collective-permute-start.2
  120.5 27.2 %collective-permute-done.2 = f32[768,384]{1,0:T(8,128)S(1)} collective-permute-done((f32[768,384]{1,0:T(8,128)}, f32[768,384]{1,0:T(8,128)S(1)}, u32[]{:S(2)}, u32[]{:S(2)}) %collective-permute-start.2) | collective-permute-done | bytes 1179680 | tf_op jit(solution)/shard_map/ppermute | solution.py:12
  147.7 6.5 %convolution_select_fusion.2 = f32[768,384]{1,0:T(8,128)} fusion(f32[768,384]{1,0:T(8,128)} %convolution_select_fusion.3, f32[768,768]{1,0:T(8,128)} %all-gather.13.cloned.1.call-done, f32[768,384]{1,0:T(8,128)S(1)} %collective-permute-done.2, pred[]{:T(512)S(6)} %ge.14), kind=kOutput, calls=%fused_computation.18 | convolution fusion | flops 2718203904 | bytes 5898241 | tf_op jit(solution)/shard_map/dot_general | solution.py:42
  154.4 1.3 collective-permute-start.3
  155.7 26.4 %collective-permute-done.3 = f32[768,384]{1,0:T(8,128)S(1)} collective-permute-done((f32[768,384]{1,0:T(8,128)}, f32[768,384]{1,0:T(8,128)S(1)}, u32[]{:S(2)}, u32[]{:S(2)}) %collective-permute-start.3) | collective-permute-done | bytes 1179680 | tf_op jit(solution)/shard_map/ppermute | solution.py:12
  182.1 6.5 %convolution_select_fusion.1 = f32[768,384]{1,0:T(8,128)} fusion(f32[768,384]{1,0:T(8,128)} %convolution_select_fusion.2, f32[768,768]{1,0:T(8,128)} %all-gather.15.cloned.1.call-done, f32[768,384]{1,0:T(8,128)S(1)} %collective-permute-done.3, pred[]{:T(512)S(6)} %ge.13), kind=kOutput, calls=%fused_computation.17 | convolution fusion | flops 2718203904 | bytes 5898241 | tf_op jit(solution)/shard_map/dot_general | solution.py:42
  188.7 1.5 collective-permute-start.4
  190.2 54.6 %collective-permute-done.4 = f32[768,384]{1,0:T(8,128)S(1)} collective-permute-done((f32[768,384]{1,0:T(8,128)}, f32[768,384]{1,0:T(8,128)S(1)}, u32[]{:S(2)}, u32[]{:S(2)}) %collective-permute-start.4) | collective-permute-done | bytes 1179680 | tf_op jit(solution)/shard_map/ppermute | solution.py:12
  244.8 5.5 %convolution_select_fusion = f32[768,384]{1,0:T(8,128)S(1)} fusion(f32[768,384]{1,0:T(8,128)} %convolution_select_fusion.1, f32[768,768]{1,0:T(8,128)} %all-gather.17.cloned.1.call-done, f32[768,384]{1,0:T(8,128)S(1)} %collective-permute-done.4, pred[]{:T(512)S(6)} %ge.12), kind=kOutput, calls=%fused_computation.16 | convolution fusion | flops 2718203904 | bytes 5898241 | tf_op jit(solution)/shard_map/dot_general | solution.py:42
  250.4 1.9 fusion.25
  252.3 20.9 %all-reduce.2.cloned.1.call-done = f32[768,128]{1,0:T(8,128)} async-done(((f32[768,128]{1,0:T(8,128)}), f32[768,128]{1,0:T(8,128)}) %all-reduce.2.cloned.1.call-update) | async-done | bytes 393232 | tf_op jit(solution)/shard_map/psum | solution.py:47
  273.2 1.3 collective-permute-start.5
  275.5 10.2 %collective-permute-done.5 = f32[768,128]{1,0:T(8,128)S(1)} collective-permute-done((f32[768,128]{1,0:T(8,128)}, f32[768,128]{1,0:T(8,128)S(1)}, u32[]{:S(2)}, u32[]{:S(2)}) %collective-permute-start.5) | collective-permute-done | bytes 393248 | tf_op jit(solution)/shard_map/ppermute | solution.py:12
  285.7 5.5 %fusion.18 = bf16[1,768,128]{2,1,0:T(8,128)(2,1)S(1)} fusion(f32[768,128]{1,0:T(8,128)S(1)} %copy-done.3, f32[768,128]{1,0:T(8,128)S(1)} %collective-permute-done.5, pred[]{:T(512)S(6)} %eq.11, f32[2,768,768]{1,2,0:T(8,128)} %copy-done), kind=kOutput, calls=%fused_computation.23 | convolution fusion | flops 906166272 | bytes 3342337 | tf_op jit(solution)/shard_map/dot_general | solution.py:52
  291.2 3.9 %fusion.4 = f32[2,1024,128]{2,1,0:T(8,128)} fusion(bf16[2,2048,768]{2,1,0:T(8,128)(2,1)} %all-gather.7.cloned.1.call-done, s32[]{:T(128)S(6)} %select_n.50, bf16[1,768,128]{2,1,0:T(8,128)(2,1)S(1)} %convert_bitcast_fusion, bf16[1,768,128]{2,1,0:T(8,128)(2,1)S(1)} %fusion.18), kind=kOutput, calls=%fused_computation.4 | convolution fusion | flops 402849792 | bytes 4587524 | tf_op jit(solution)/shard_map/shm,smc->shc/dot_general | solution.py:58
  (36 shorter events, 5.4 us)
Async XLA Ops:
  6.5 1.9 copy-start.1
  6.5 40.5 %all-gather.7.cloned.1.call-start = ((), (), s32[]{:S(2)}) async-start(), calls=%async_computation | async-start | bytes 9437184 | tf_op jit(solution)/shard_map/all_gather | solution.py:28
  7.3 39.7 %copy-start.4 = (f32[2,768]{1,0:T(2,128)S(1)}, f32[2,768]{1,0:T(2,128)}, u32[]{:S(2)}) copy-start(f32[2,768]{1,0:T(2,128)} %param.6) | copy-start | bytes 18436
  7.3 54.3 %all-gather.9.cloned.1.call-start = ((), (), s32[]{:S(2)}) async-start(), calls=%async_computation.1 | async-start | bytes 4718592 | tf_op jit(solution)/shard_map/all_gather | solution.py:29
  8.6 37.2 %collective-permute-start = (bf16[2048,384]{1,0:T(8,128)(2,1)S(1)}, bf16[2048,384]{1,0:T(8,128)(2,1)S(1)}, u32[]{:S(2)}, u32[]{:S(2)}) collective-permute-start(bf16[2048,384]{1,0:T(8,128)(2,1)S(1)} %slice_bitcast_fusion.2), channel_id=1, source_target_pairs={{0,2},{2,4},{4,6},{6,8},{8,10},{10,12},{12,14},{14,16},{16,18},{18... | collective-permute-start | bytes 4718600 | tf_op jit(solution)/shard_map/ppermute | solution.py:12
  45.8 1.1 copy-start.2
  46.9 65.7 %all-gather.11.cloned.1.call-start = ((), (), s32[]{:S(2)}) async-start(), calls=%async_computation.2 | async-start | bytes 3538944 | tf_op jit(solution)/shard_map/all_gather | solution.py:43
  47.0 14.6 %slice-start = ((bf16[2,2048,768]{2,1,0:T(8,128)(2,1)}), bf16[1,2048,768]{2,1,0:T(8,128)(2,1)S(1)}, s32[]{:S(2)}) async-start(bf16[2,2048,768]{2,1,0:T(8,128)(2,1)} %all-gather.7.cloned.1.call-done), calls=%async_computation.7 | async-start | bytes 6291456 | tf_op jit(solution)/shard_map/slice | solution.py:31
  72.2 2.2 copy-start
  83.1 64.6 %all-gather.13.cloned.1.call-start = ((), (), s32[]{:S(2)}) async-start(), calls=%async_computation.3 | async-start | bytes 3538944 | tf_op jit(solution)/shard_map/all_gather | solution.py:43
  83.2 29.4 %collective-permute-start.1 = (f32[768,384]{1,0:T(8,128)}, f32[768,384]{1,0:T(8,128)S(1)}, u32[]{:S(2)}, u32[]{:S(2)}) collective-permute-start(f32[768,384]{1,0:T(8,128)} %fusion.6), channel_id=1, source_target_pairs={{0,2},{2,4},{4,6},{6,8},{8,10},{10,12},{12,14},{14,16},{16,18},{18... | collective-permute-start | bytes 3538952 | tf_op jit(solution)/shard_map/ppermute | solution.py:12
  119.2 62.9 %all-gather.15.cloned.1.call-start = ((), (), s32[]{:S(2)}) async-start(), calls=%async_computation.4 | async-start | bytes 3538944 | tf_op jit(solution)/shard_map/all_gather | solution.py:43
  119.2 28.5 %collective-permute-start.2 = (f32[768,384]{1,0:T(8,128)}, f32[768,384]{1,0:T(8,128)S(1)}, u32[]{:S(2)}, u32[]{:S(2)}) collective-permute-start(f32[768,384]{1,0:T(8,128)} %convolution_select_fusion.3), channel_id=1, source_target_pairs={{0,4},{2,6},{4,8},{6,10},{8,12},{10,14},{12,16},{14,18},{16,20},{1... | collective-permute-start | bytes 3538952 | tf_op jit(solution)/shard_map/ppermute | solution.py:12
  154.3 90.5 %all-gather.17.cloned.1.call-start = ((), (), s32[]{:S(2)}) async-start(), calls=%async_computation.5 | async-start | bytes 3538944 | tf_op jit(solution)/shard_map/all_gather | solution.py:43
  154.4 27.7 %collective-permute-start.3 = (f32[768,384]{1,0:T(8,128)}, f32[768,384]{1,0:T(8,128)S(1)}, u32[]{:S(2)}, u32[]{:S(2)}) collective-permute-start(f32[768,384]{1,0:T(8,128)} %convolution_select_fusion.2), channel_id=1, source_target_pairs={{0,8},{2,10},{4,12},{6,14},{8,16},{10,18},{12,20},{14,22},{16,24},... | collective-permute-start | bytes 3538952 | tf_op jit(solution)/shard_map/ppermute | solution.py:12
  188.6 84.5 %all-reduce.2.cloned.1.call-start = ((), (), s32[]{:S(2)}) async-start(), calls=%async_computation.6 | async-start | bytes 786432 | tf_op jit(solution)/shard_map/psum | solution.py:47
  188.7 56.1 %collective-permute-start.4 = (f32[768,384]{1,0:T(8,128)}, f32[768,384]{1,0:T(8,128)S(1)}, u32[]{:S(2)}, u32[]{:S(2)}) collective-permute-start(f32[768,384]{1,0:T(8,128)} %convolution_select_fusion.1), channel_id=1, source_target_pairs={{0,16},{2,18},{4,20},{6,22},{8,24},{10,26},{12,28},{14,30},{1,17},... | collective-permute-start | bytes 3538952 | tf_op jit(solution)/shard_map/ppermute | solution.py:12
  190.2 60.2 %copy-start.3 = (f32[768,128]{1,0:T(8,128)S(1)}, f32[768,128]{1,0:T(8,128)}, u32[]{:S(2)}) copy-start(f32[768,128]{1,0:T(8,128)} %param.7) | copy-start | bytes 1179652
  273.2 12.5 %collective-permute-start.5 = (f32[768,128]{1,0:T(8,128)}, f32[768,128]{1,0:T(8,128)S(1)}, u32[]{:S(2)}, u32[]{:S(2)}) collective-permute-start(f32[768,128]{1,0:T(8,128)} %all-reduce.2.cloned.1.call-done), channel_id=1, source_target_pairs={{0,2},{2,4},{4,6},{6,8},{8,10},{10,12},{12,14},{14,16},{16,18},{18... | collective-permute-start | bytes 1179656 | tf_op jit(solution)/shard_map/ppermute | solution.py:12
Sparse Core Ops, SparseCore 0:
  8.9 18.1 all-gather.6
  47.1 14.4 all-gather.8
  83.2 12.1 all-gather.10
  119.3 12.9 all-gather.12
  154.4 14.7 all-gather.14
  188.7 15.5 all-gather.16
  252.4 20.7 all-reduce.1
where the time goes:
time: 305 us; the launch traced here: 302 us
  waiting for transfers between devices  219 us (72%)
  matrix products  54.9 us (18%)
  between operations  13.7 us (4%)
  starting transfers between devices  8.21 us (3%)
  local copies, waits for them, and re-layouts  4.66 us (2%)
    ppermute x6, waiting for transfers between devices, from_behind(): lax.ppermute(value, axis, [(source, source + steps) for source in range(i...  182 us
    dot_general x4, matrix products, on_device(): jnp.dot(lax.all_gather(prefix, 'chip', axis=1, tiled=True), earlier_part,...  25.1 us
    psum x1, waiting for transfers between devices, on_device(): reached = lax.psum(jnp.dot(prefix, source_rows, precision=highest), 'chip')  20.9 us
    all_gather x1, waiting for transfers between devices, on_device(): lax.all_gather(earlier_half, 'chip', axis=1, tiled=True)  14.5 us
    dot_general x1, matrix products, on_device(): jnp.einsum('shm,shn->smn', tables, previous, preferred_element_type=jnp.f...  9.85 us
    dot_general x1, matrix products, on_device(): prefix = jnp.dot(matrices[segment], prefix, precision=highest)  8.7 us
    ppermute x6, starting transfers between devices, from_behind(): lax.ppermute(value, axis, [(source, source + steps) for source in range(i...  7.96 us
  transfers between devices with their start and end apart: 13, of which 8 were waited for; matrix products, arithmetic and copies ran while one was open for 0% of the time, Pallas kernels for 0%

commit v1 on v0

v1 whole, which is shorter than its diff:
```python
import functools

import jax
import jax.numpy as jnp
from jax import lax
from jax.experimental import pallas as pl
from jax.experimental.pallas import tpu as pltpu
from jax.sharding import PartitionSpec as P

MESH = pl.DeviceIdType.MESH
BF16, F32 = jnp.bfloat16, jnp.float32


def contract(a, b, da, db):
    return lax.dot_general(a, b, (((da,), (db,)), ((), ())), preferred_element_type=F32)


def split(x):
    hi = x.astype(BF16)
    return hi, (x - hi.astype(F32)).astype(BF16)


def times(x, w_hi, w_lo):
    rows = x.shape[0]
    hi, lo = split(x)
    both = contract(jnp.concatenate([hi, lo], axis=0), w_hi[...], 1, 0)
    return both[:rows] + (both[rows:] + contract(hi, w_lo[...], 1, 0))


def kernel(
    n, pieces, chunks,
    tab, att, exc, out,
    T, E, acc, m1, m0, pr, arrive, leave, rounded,
    load_sem, gat_s, gat_r, ear_s, ear_r, mat_s, mat_r, ch_s, ch_r, rd_s, rd_r,
):
    pos, core = lax.axis_index("range"), lax.axis_index("chip")
    other = 1 - core
    segs, heights, half = tab.shape
    modes = 2 * half
    own_cols = pl.ds(pl.multiple_of(core * half, 128), half)
    own_rows = pl.ds(pl.multiple_of(core * half, 128), half)
    partner, ahead, behind = (pos, other), (pos + 1, core), (pos - 1, core)
    has_next, has_prev = pos < n - 1, pos > 0

    loads = [
        pltpu.make_async_copy(tab.at[s], T.at[s, :, own_cols], load_sem.at[s]) for s in range(segs)
    ]
    for c in loads:
        c.start()
    barrier = pltpu.get_barrier_semaphore()
    pl.semaphore_signal(barrier, inc=1, device_id=partner, device_id_type=MESH)

    @pl.when(has_next)
    def _():
        pl.semaphore_signal(barrier, inc=1, device_id=ahead, device_id_type=MESH)

    @pl.when(has_prev)
    def _():
        pl.semaphore_signal(barrier, inc=1, device_id=behind, device_id_type=MESH)

    pl.semaphore_wait(barrier, 1 + has_next.astype(jnp.int32) + has_prev.astype(jnp.int32))

    def remote(src, dst, s, r, to):
        return pltpu.make_async_remote_copy(
            src_ref=src, dst_ref=dst, send_sem=s, recv_sem=r, device_id=to, device_id_type=MESH
        )

    gathers = [
        remote(tab.at[s], T.at[s, :, own_cols], gat_s.at[s], gat_r.at[s], partner)
        for s in range(segs)
    ]
    for c in gathers:
        c.start()
    size = heights // pieces

    def piece(i):
        rows = pl.ds(pl.multiple_of(i * size, 128), size)
        return remote(tab.at[segs - 1, rows], E.at[rows], ear_s.at[i], ear_r.at[i], ahead), rows

    @pl.when(has_next)
    def _():
        @pl.loop(0, pieces)
        def _(i):
            piece(i)[0].start()

    damp0, damp1 = jnp.exp(-att[0:1, :]), jnp.exp(-att[1:2, :])
    for c in loads:
        c.wait()
    for c in gathers:
        c.wait()

    @pl.loop(0, 2)
    def _(j):
        rows = pl.ds(pl.multiple_of(j * half, 128), half)
        m1[0, rows], m1[1, rows] = split(contract(T[0, :, rows], T[1], 0, 0) * damp1)

    @pl.when(jnp.logical_not(has_prev))
    def _():
        r = lax.broadcasted_iota(jnp.int32, (half, modes), 0) + core * half
        c = lax.broadcasted_iota(jnp.int32, (half, modes), 1)
        acc[...] = jnp.where(r == c, 1.0, 0.0).astype(F32)
        columns = exc[...].T
        count = chunks * arrive.shape[1]
        for k in range(2):
            @pl.when(core == k)
            def _():
                mine = columns[k * count:(k + 1) * count]
                arrive[...] = mine.reshape(arrive.shape)

    @pl.when(has_prev)
    def _():
        acc[...] = jnp.zeros_like(acc)

        @pl.loop(0, pieces)
        def _(i):
            copy, rows = piece(i)
            copy.wait_recv()
            acc[...] += contract(E[rows], T[0, rows], 0, 0)

    scaled = acc[...] * damp0
    m0[0, own_rows], m0[1, own_rows] = split(scaled)
    product = times(scaled, m1.at[0], m1.at[1])
    pr[0, own_rows], pr[1, own_rows] = split(product)
    mats = [
        remote(ref.at[k, own_rows], ref.at[k, own_rows], mat_s.at[2 * i + k], mat_r.at[2 * i + k], partner)
        for i, ref in enumerate((pr, m0)) for k in range(2)
    ]
    for c in mats:
        c.start()
    for c in mats[:2]:
        c.wait()

    def hop(k):
        return remote(leave.at[k], arrive.at[k], ch_s.at[k], ch_r.at[k], ahead)

    @pl.loop(0, chunks)
    def _(k):
        @pl.when(has_prev)
        def _():
            hop(k).wait_recv()

        leave[k] = times(arrive[k], pr.at[0], pr.at[1])

        @pl.when(has_next)
        def _():
            hop(k).start()

    for c in mats[2:]:
        c.wait()
    count = chunks * arrive.shape[1]
    mine = pl.ds(pl.multiple_of(core * count, 16), count)
    rounded[1, mine] = leave[...].reshape(count, modes).astype(BF16)
    late = remote(rounded.at[1, mine], rounded.at[1, mine], rd_s.at[1], rd_r.at[1], partner)
    late.start()
    rounded[0, mine] = times(arrive[...].reshape(count, modes), m0.at[0], m0.at[1]).astype(BF16)
    early = remote(rounded.at[0, mine], rounded.at[0, mine], rd_s.at[0], rd_r.at[0], partner)
    early.start()
    rows = heights // 2
    first = pl.multiple_of(core * rows, 128)
    for s, copy in ((1, late), (0, early)):
        copy.wait()
        out[s] = contract(T[s, pl.ds(first, rows)], rounded[s], 1, 1)

    @pl.when(has_next)
    def _():
        @pl.loop(0, pieces)
        def _(i):
            piece(i)[0].wait_send()

        @pl.loop(0, chunks)
        def _(k):
            hop(k).wait_send()


def solution(mesh):
    n, cores = mesh.shape["range"], mesh.shape["chip"]

    def on_device(tab, att, exc):
        segs, heights, half = tab.shape
        modes, sources = exc.shape
        pieces, chunks = 8, 4
        rows = sources // cores // chunks
        dma = pltpu.SemaphoreType.DMA
        vmem = pl.BlockSpec(memory_space=pltpu.VMEM)
        return pl.pallas_call(
            functools.partial(kernel, n, pieces, chunks),
            out_shape=jax.ShapeDtypeStruct((segs, heights // cores, sources), F32),
            in_specs=[pl.BlockSpec(memory_space=pl.ANY), vmem, vmem],
            out_specs=vmem,
            scratch_shapes=[
                pltpu.VMEM((segs, heights, modes), BF16),
                pltpu.VMEM((heights, half), BF16),
                pltpu.VMEM((half, modes), F32),
                pltpu.VMEM((2, modes, modes), BF16),
                pltpu.VMEM((2, modes, modes), BF16),
                pltpu.VMEM((2, modes, modes), BF16),
                pltpu.VMEM((chunks, rows, modes), F32),
                pltpu.VMEM((chunks, rows, modes), F32),
                pltpu.VMEM((segs, sources, modes), BF16),
                dma((segs,)),
                dma((segs,)), dma((segs,)),
                dma((pieces,)), dma((pieces,)),
                dma((4,)), dma((4,)),
                dma((chunks,)), dma((chunks,)),
                dma((2,)), dma((2,)),
            ],
            compiler_params=pltpu.CompilerParams(
                collective_id=0, has_side_effects=True, vmem_limit_bytes=60 * 2**20
            ),
        )(tab, att, exc)

    return jax.shard_map(
        on_device, mesh=mesh,
        in_specs=(P("range", None, "chip"), P("range", None), P()),
        out_specs=P("range", "chip", None), check_vma=False,
    )
```

time: 305 us -> 106 us (0.35)
  waiting for transfers between devices: 219 us -> 0 us
  Pallas kernels: 0 us -> 103 us
  matrix products: 54.9 us -> 0 us
  between operations: 13.7 us -> 0.01 us
  starting transfers between devices: 8.21 us -> 0 us
    ppermute x6 -> x0, waiting for transfers between devices: 182 us -> none  [from_behind(): lax.ppermute(value, axis, [(source, source + steps) for source in range(i...]
    pallas_call x0 -> x1, Pallas kernels: none -> 103 us  [on_device(): pl.pallas_call(functools.partial(kernel, n, pieces, chunks), out_shape=ja...]
    dot_general x9 -> x0, matrix products: 54.9 us -> none  [the longest x4 25.1 us: on_device(): jnp.dot(lax.all_gather(prefix, 'chip', axis=1, tiled=True), earlier_part,...]
    psum x1 -> x0, waiting for transfers between devices: 20.9 us -> none  [on_device(): reached = lax.psum(jnp.dot(prefix, source_rows, precision=highest), 'chip')]
    all_gather x6 -> x0, waiting for transfers between devices: 14.6 us -> none  [the longest x1 14.5 us: on_device(): lax.all_gather(earlier_half, 'chip', axis=1, tiled=True)]
    ppermute x6 -> x0, starting transfers between devices: 7.96 us -> none  [from_behind(): lax.ppermute(value, axis, [(source, source + steps) for source in range(i...]
  transfers between devices with their start and end apart: 13 -> 0, of which waited for: 8 -> 0; matrix products, arithmetic and copies ran while one was open for 0% -> 0% of each run, Pallas kernels for 0% -> 0%
where the time goes in v1:
time: 106 us; the launch traced here: 105 us
  Pallas kernels  103 us (97%)
  local copies, waits for them, and re-layouts  2.26 us (2%)
    pallas_call x1, Pallas kernels, on_device(): pl.pallas_call(functools.partial(kernel, n, pieces, chunks), out_shape=ja...  103 us
    unnamed x1, local copies, waits for them, and re-layouts  2.26 us

profile of v1, /device:TPU:31, one launch (start us, length us, event | category | flops | bytes accessed | tf_op | source)
XLA Modules:
  0.0 105.4 jit_solution(6018371179824676809)
XLA Ops:
  0.0 103.1 %shard_map.37 = f32[2,1024,128]{2,1,0:T(8,128)} custom-call(bf16[2,2048,384]{2,1,0:T(8,128)(2,1)} %tab.1, f32[2,768]{1,0:T(2,128)} %att.1, f32[768,128]{1,0:T(8,128)} %exc.1), custom_call_target="tpu_custom_call" | custom-call | tf_op jit(solution)/shard_map/pallas_call | solution.py:185
  103.1 2.3 %copy.5 = f32[2,1024,128]{2,1,0:T(8,128)} copy(f32[2,1024,128]{2,1,0:T(8,128)} %shard_map.37) | data formatting | bytes 2097152

commit v2 on v1

--- a/solution.py
+++ b/solution.py
@@ -20,17 +20,27 @@
     return hi, (x - hi.astype(F32)).astype(BF16)
 
 
+def stacked(x):
+    hi = x.astype(BF16).astype(F32)
+    return jnp.concatenate([hi, x - hi], axis=0).astype(BF16)
+
+
 def times(x, w_hi, w_lo):
     rows = x.shape[0]
-    hi, lo = split(x)
-    both = contract(jnp.concatenate([hi, lo], axis=0), w_hi[...], 1, 0)
-    return both[:rows] + (both[rows:] + contract(hi, w_lo[...], 1, 0))
+    both = contract(stacked(x), w_hi[...], 1, 0)
+    return both[:rows] + (both[rows:] + contract(x.astype(BF16), w_lo[...], 1, 0))
+
+
+def times_table(x, table, dim):
+    rows = x.shape[0]
+    both = contract(stacked(x), table, 1, dim)
+    return both[:rows] + both[rows:]
 
 
 def kernel(
-    n, pieces, chunks,
+    n, wide, pieces, chunks,
     tab, att, exc, out,
-    T, E, acc, m1, m0, pr, arrive, leave, rounded,
+    T, E, acc, m1, m0, pr, arrive, leave, arrive_u, leave_u, early_a, rounded,
     load_sem, gat_s, gat_r, ear_s, ear_r, mat_s, mat_r, ch_s, ch_r, rd_s, rd_r,
 ):
     pos, core = lax.axis_index("range"), lax.axis_index("chip")
@@ -41,6 +51,8 @@
     own_rows = pl.ds(pl.multiple_of(core * half, 128), half)
     partner, ahead, behind = (pos, other), (pos + 1, core), (pos - 1, core)
     has_next, has_prev = pos < n - 1, pos > 0
+    wide_out, narrow_out = pos < wide, jnp.logical_and(pos >= wide, has_next)
+    wide_in, narrow_in = jnp.logical_and(has_prev, pos <= wide), pos > wide
 
     loads = [
         pltpu.make_async_copy(tab.at[s], T.at[s, :, own_cols], load_sem.at[s]) for s in range(segs)
@@ -77,7 +89,7 @@
         rows = pl.ds(pl.multiple_of(i * size, 128), size)
         return remote(tab.at[segs - 1, rows], E.at[rows], ear_s.at[i], ear_r.at[i], ahead), rows
 
-    @pl.when(has_next)
+    @pl.when(narrow_out)
     def _():
         @pl.loop(0, pieces)
         def _(i):
@@ -94,20 +106,51 @@
         rows = pl.ds(pl.multiple_of(j * half, 128), half)
         m1[0, rows], m1[1, rows] = split(contract(T[0, :, rows], T[1], 0, 0) * damp1)
 
+    count = chunks * arrive.shape[1]
+
+    def hop(k):
+        return remote(leave.at[k], arrive.at[k], ch_s.at[k], ch_r.at[k], ahead)
+
+    def wide_hop(k):
+        return remote(leave_u.at[k], arrive_u.at[k], ch_s.at[k], ch_r.at[k], ahead)
+
+    def send(k):
+        @pl.when(wide_out)
+        def _():
+            leave_u[k] = times_table(leave[k], T[1], 1)
+            wide_hop(k).start()
+
+        @pl.when(narrow_out)
+        def _():
+            hop(k).start()
+
     @pl.when(jnp.logical_not(has_prev))
     def _():
-        r = lax.broadcasted_iota(jnp.int32, (half, modes), 0) + core * half
-        c = lax.broadcasted_iota(jnp.int32, (half, modes), 1)
-        acc[...] = jnp.where(r == c, 1.0, 0.0).astype(F32)
         columns = exc[...].T
-        count = chunks * arrive.shape[1]
         for k in range(2):
             @pl.when(core == k)
             def _():
-                mine = columns[k * count:(k + 1) * count]
-                arrive[...] = mine.reshape(arrive.shape)
-
-    @pl.when(has_prev)
+                start = columns[k * count:(k + 1) * count] * damp0
+                early_a[...] = start.reshape(early_a.shape)
+
+        start = early_a[...].reshape(count, modes)
+        leave[...] = times(start, m1.at[0], m1.at[1]).reshape(leave.shape)
+
+        @pl.loop(0, chunks)
+        def _(k):
+            send(k)
+
+    @pl.when(wide_in)
+    def _():
+        @pl.loop(0, chunks)
+        def _(k):
+            wide_hop(k).wait_recv()
+            value = times_table(arrive_u[k], T[0], 0) * damp0
+            early_a[k] = value
+            leave[k] = times(value, m1.at[0], m1.at[1])
+            send(k)
+
+    @pl.when(narrow_in)
     def _():
         acc[...] = jnp.zeros_like(acc)
 
@@ -117,42 +160,35 @@
             copy.wait_recv()
             acc[...] += contract(E[rows], T[0, rows], 0, 0)
 
-    scaled = acc[...] * damp0
-    m0[0, own_rows], m0[1, own_rows] = split(scaled)
-    product = times(scaled, m1.at[0], m1.at[1])
-    pr[0, own_rows], pr[1, own_rows] = split(product)
-    mats = [
-        remote(ref.at[k, own_rows], ref.at[k, own_rows], mat_s.at[2 * i + k], mat_r.at[2 * i + k], partner)
-        for i, ref in enumerate((pr, m0)) for k in range(2)
-    ]
-    for c in mats:
-        c.start()
-    for c in mats[:2]:
-        c.wait()
-
-    def hop(k):
-        return remote(leave.at[k], arrive.at[k], ch_s.at[k], ch_r.at[k], ahead)
-
-    @pl.loop(0, chunks)
-    def _(k):
-        @pl.when(has_prev)
-        def _():
+        scaled = acc[...] * damp0
+        m0[0, own_rows], m0[1, own_rows] = split(scaled)
+        product = times(scaled, m1.at[0], m1.at[1])
+        pr[0, own_rows], pr[1, own_rows] = split(product)
+        mats = [
+            remote(ref.at[k, own_rows], ref.at[k, own_rows], mat_s.at[2 * i + k], mat_r.at[2 * i + k], partner)
+            for i, ref in enumerate((pr, m0)) for k in range(2)
+        ]
+        for c in mats:
+            c.start()
+        for c in mats[:2]:
+            c.wait()
+
+        @pl.loop(0, chunks)
+        def _(k):
             hop(k).wait_recv()
-
-        leave[k] = times(arrive[k], pr.at[0], pr.at[1])
-
-        @pl.when(has_next)
-        def _():
-            hop(k).start()
-
-    for c in mats[2:]:
-        c.wait()
-    count = chunks * arrive.shape[1]
+            leave[k] = times(arrive[k], pr.at[0], pr.at[1])
+            send(k)
+
+        for c in mats[2:]:
+            c.wait()
+        value = times(arrive[...].reshape(count, modes), m0.at[0], m0.at[1])
+        early_a[...] = value.reshape(early_a.shape)
+
     mine = pl.ds(pl.multiple_of(core * count, 16), count)
     rounded[1, mine] = leave[...].reshape(count, modes).astype(BF16)
     late = remote(rounded.at[1, mine], rounded.at[1, mine], rd_s.at[1], rd_r.at[1], partner)
     late.start()
-    rounded[0, mine] = times(arrive[...].reshape(count, modes), m0.at[0], m0.at[1]).astype(BF16)
+    rounded[0, mine] = early_a[...].reshape(count, modes).astype(BF16)
     early = remote(rounded.at[0, mine], rounded.at[0, mine], rd_s.at[0], rd_r.at[0], partner)
     early.start()
     rows = heights // 2
@@ -161,7 +197,7 @@
         copy.wait()
         out[s] = contract(T[s, pl.ds(first, rows)], rounded[s], 1, 1)
 
-    @pl.when(has_next)
+    @pl.when(narrow_out)
     def _():
         @pl.loop(0, pieces)
         def _(i):
@@ -171,6 +207,12 @@
         def _(k):
             hop(k).wait_send()
 
+    @pl.when(wide_out)
+    def _():
+        @pl.loop(0, chunks)
+        def _(k):
+            wide_hop(k).wait_send()
+
 
 def solution(mesh):
     n, cores = mesh.shape["range"], mesh.shape["chip"]
@@ -178,12 +220,12 @@
     def on_device(tab, att, exc):
         segs, heights, half = tab.shape
         modes, sources = exc.shape
-        pieces, chunks = 8, 4
+        wide, pieces, chunks = min(4, n - 1), 8, 8
         rows = sources // cores // chunks
         dma = pltpu.SemaphoreType.DMA
         vmem = pl.BlockSpec(memory_space=pltpu.VMEM)
         return pl.pallas_call(
-            functools.partial(kernel, n, pieces, chunks),
+            functools.partial(kernel, n, wide, pieces, chunks),
             out_shape=jax.ShapeDtypeStruct((segs, heights // cores, sources), F32),
             in_specs=[pl.BlockSpec(memory_space=pl.ANY), vmem, vmem],
             out_specs=vmem,
@@ -195,6 +237,9 @@
                 pltpu.VMEM((2, modes, modes), BF16),
                 pltpu.VMEM((2, modes, modes), BF16),
                 pltpu.VMEM((chunks, rows, modes), F32),
+                pltpu.VMEM((chunks, rows, modes), F32),
+                pltpu.VMEM((chunks, rows, heights), F32),
+                pltpu.VMEM((chunks, rows, heights), F32),
                 pltpu.VMEM((chunks, rows, modes), F32),
                 pltpu.VMEM((segs, sources, modes), BF16),
                 dma((segs,)),

time: 106 us -> 92.9 us (0.88)
  Pallas kernels: 103 us -> 90.4 us
    pallas_call x1, Pallas kernels: 103 us -> 90.4 us  [on_device(): pl.pallas_call(functools.partial(kernel, n, wide, pieces, chunks), out_sh...]
where the time goes in v2:
time: 92.9 us; the launch traced here: 92.7 us
  Pallas kernels  90.4 us (97%)
  local copies, waits for them, and re-layouts  2.26 us (2%)
    pallas_call x1, Pallas kernels, on_device(): pl.pallas_call(functools.partial(kernel, n, wide, pieces, chunks), out_sh...  90.4 us
    unnamed x1, local copies, waits for them, and re-layouts  2.26 us

profile of v2, /device:TPU:31, one launch (start us, length us, event | category | flops | bytes accessed | tf_op | source)
XLA Modules:
  0.0 92.7 jit_solution(2339947544742479396)
XLA Ops:
  0.0 90.4 %shard_map.37 = f32[2,1024,128]{2,1,0:T(8,128)} custom-call(bf16[2,2048,384]{2,1,0:T(8,128)(2,1)} %tab.1, f32[2,768]{1,0:T(2,128)} %att.1, f32[768,128]{1,0:T(8,128)} %exc.1), custom_call_target="tpu_custom_call" | custom-call | tf_op jit(solution)/shard_map/pallas_call | solution.py:227
  90.5 2.3 %copy.5 = f32[2,1024,128]{2,1,0:T(8,128)} copy(f32[2,1024,128]{2,1,0:T(8,128)} %shard_map.37) | data formatting | bytes 2097152

commit v3 on v2

--- a/solution.py
+++ b/solution.py
@@ -40,7 +40,7 @@
 def kernel(
     n, wide, pieces, chunks,
     tab, att, exc, out,
-    T, E, acc, m1, m0, pr, arrive, leave, arrive_u, leave_u, early_a, rounded,
+    T, E, acc, m1, m0, pr, arrive, leave, arrive_u, leave_u, early_a, late_r, rounded,
     load_sem, gat_s, gat_r, ear_s, ear_r, mat_s, mat_r, ch_s, ch_r, rd_s, rd_r,
 ):
     pos, core = lax.axis_index("range"), lax.axis_index("chip")
@@ -101,10 +101,12 @@
     for c in gathers:
         c.wait()
 
-    @pl.loop(0, 2)
-    def _(j):
-        rows = pl.ds(pl.multiple_of(j * half, 128), half)
-        m1[0, rows], m1[1, rows] = split(contract(T[0, :, rows], T[1], 0, 0) * damp1)
+    @pl.when(has_prev)
+    def _():
+        @pl.loop(0, 2)
+        def _(j):
+            rows = pl.ds(pl.multiple_of(j * half, 128), half)
+            m1[0, rows], m1[1, rows] = split(contract(T[0, :, rows], T[1], 0, 0) * damp1)
 
     count = chunks * arrive.shape[1]
 
@@ -113,6 +115,10 @@
 
     def wide_hop(k):
         return remote(leave_u.at[k], arrive_u.at[k], ch_s.at[k], ch_r.at[k], ahead)
+
+    def late(k):
+        mine = late_r.at[core, k]
+        return remote(mine, mine, rd_s.at[k], rd_r.at[k], partner)
 
     def send(k):
         @pl.when(wide_out)
@@ -123,6 +129,9 @@
         @pl.when(narrow_out)
         def _():
             hop(k).start()
+
+        late_r[core, k] = leave[k].astype(BF16)
+        late(k).start()
 
     @pl.when(jnp.logical_not(has_prev))
     def _():
@@ -134,7 +143,8 @@
                 early_a[...] = start.reshape(early_a.shape)
 
         start = early_a[...].reshape(count, modes)
-        leave[...] = times(start, m1.at[0], m1.at[1]).reshape(leave.shape)
+        value = times_table(times_table(start, T[0], 1), T[1], 0) * damp1
+        leave[...] = value.reshape(leave.shape)
 
         @pl.loop(0, chunks)
         def _(k):
@@ -185,17 +195,19 @@
         early_a[...] = value.reshape(early_a.shape)
 
     mine = pl.ds(pl.multiple_of(core * count, 16), count)
-    rounded[1, mine] = leave[...].reshape(count, modes).astype(BF16)
-    late = remote(rounded.at[1, mine], rounded.at[1, mine], rd_s.at[1], rd_r.at[1], partner)
-    late.start()
-    rounded[0, mine] = early_a[...].reshape(count, modes).astype(BF16)
-    early = remote(rounded.at[0, mine], rounded.at[0, mine], rd_s.at[0], rd_r.at[0], partner)
+    rounded[mine] = early_a[...].reshape(count, modes).astype(BF16)
+    early = remote(rounded.at[mine], rounded.at[mine], rd_s.at[chunks], rd_r.at[chunks], partner)
     early.start()
     rows = heights // 2
     first = pl.multiple_of(core * rows, 128)
-    for s, copy in ((1, late), (0, early)):
-        copy.wait()
-        out[s] = contract(T[s, pl.ds(first, rows)], rounded[s], 1, 1)
+
+    @pl.loop(0, chunks)
+    def _(k):
+        late(k).wait()
+
+    out[1] = contract(T[1, pl.ds(first, rows)], late_r[...].reshape(rounded.shape), 1, 1)
+    early.wait()
+    out[0] = contract(T[0, pl.ds(first, rows)], rounded[...], 1, 1)
 
     @pl.when(narrow_out)
     def _():
@@ -226,7 +238,7 @@
         vmem = pl.BlockSpec(memory_space=pltpu.VMEM)
         return pl.pallas_call(
             functools.partial(kernel, n, wide, pieces, chunks),
-            out_shape=jax.ShapeDtypeStruct((segs, heights // cores, sources), F32),
+            out_shape=pltpu.VMEM((segs, heights // cores, sources), F32),
             in_specs=[pl.BlockSpec(memory_space=pl.ANY), vmem, vmem],
             out_specs=vmem,
             scratch_shapes=[
@@ -241,13 +253,14 @@
                 pltpu.VMEM((chunks, rows, heights), F32),
                 pltpu.VMEM((chunks, rows, heights), F32),
                 pltpu.VMEM((chunks, rows, modes), F32),
-                pltpu.VMEM((segs, sources, modes), BF16),
+                pltpu.VMEM((cores, chunks, rows, modes), BF16),
+                pltpu.VMEM((sources, modes), BF16),
                 dma((segs,)),
                 dma((segs,)), dma((segs,)),
                 dma((pieces,)), dma((pieces,)),
                 dma((4,)), dma((4,)),
                 dma((chunks,)), dma((chunks,)),
-                dma((2,)), dma((2,)),
+                dma((chunks + 1,)), dma((chunks + 1,)),
             ],
             compiler_params=pltpu.CompilerParams(
                 collective_id=0, has_side_effects=True, vmem_limit_bytes=60 * 2**20

time: 92.9 us -> 88.4 us (0.952)
  Pallas kernels: 90.4 us -> 87.2 us
  local copies, waits for them, and re-layouts: 2.26 us -> 0.97 us
    pallas_call x1, Pallas kernels: 90.4 us -> 87.2 us  [on_device(): pl.pallas_call(functools.partial(kernel, n, wide, pieces, chunks), out_sh...]
    unnamed x1, local copies, waits for them, and re-layouts: 2.26 us -> 0.97 us
where the time goes in v3:
time: 88.4 us; the launch traced here: 88.2 us
  Pallas kernels  87.2 us (99%)
  local copies, waits for them, and re-layouts  0.97 us (1%)
    pallas_call x1, Pallas kernels, on_device(): pl.pallas_call(functools.partial(kernel, n, wide, pieces, chunks), out_sh...  87.2 us

profile of v3, /device:TPU:31, one launch (start us, length us, event | category | flops | bytes accessed | tf_op | source)
XLA Modules:
  0.0 88.2 jit_solution(10746820030924445181)
XLA Ops:
  0.0 87.2 %shard_map.37 = f32[2,1024,128]{2,1,0:T(8,128)S(1)} custom-call(bf16[2,2048,384]{2,1,0:T(8,128)(2,1)} %tab.1, f32[2,768]{1,0:T(2,128)} %att.1, f32[768,128]{1,0:T(8,128)} %exc.1), custom_call_target="tpu_custom_call" | custom-call | tf_op jit(solution)/shard_map/pallas_call | solution.py:239
  87.2 1.0 %copy.5 = f32[2,1024,128]{2,1,0:T(8,128)} copy(f32[2,1024,128]{2,1,0:T(8,128)S(1)} %shard_map.37) | data formatting | bytes 2097152

commit v4 on v3

--- a/solution.py
+++ b/solution.py
@@ -41,7 +41,7 @@
     n, wide, pieces, chunks,
     tab, att, exc, out,
     T, E, acc, m1, m0, pr, arrive, leave, arrive_u, leave_u, early_a, late_r, rounded,
-    load_sem, gat_s, gat_r, ear_s, ear_r, mat_s, mat_r, ch_s, ch_r, rd_s, rd_r,
+    load_sem, gat_s, gat_r, ear_s, ear_r, mat_s, mat_r, ch_s, ch_r, wd_s, wd_r, rd_s, rd_r,
 ):
     pos, core = lax.axis_index("range"), lax.axis_index("chip")
     other = 1 - core
@@ -113,8 +113,11 @@
     def hop(k):
         return remote(leave.at[k], arrive.at[k], ch_s.at[k], ch_r.at[k], ahead)
 
-    def wide_hop(k):
-        return remote(leave_u.at[k], arrive_u.at[k], ch_s.at[k], ch_r.at[k], ahead)
+    parts = leave_u.shape[0]
+    depth = heights // parts
+
+    def wide_hop(k, p):
+        return remote(leave_u.at[p, k], arrive_u.at[p, k], wd_s.at[p, k], wd_r.at[p, k], ahead)
 
     def late(k):
         mine = late_r.at[core, k]
@@ -123,8 +126,9 @@
     def send(k):
         @pl.when(wide_out)
         def _():
-            leave_u[k] = times_table(leave[k], T[1], 1)
-            wide_hop(k).start()
+            for p in range(parts):
+                leave_u[p, k] = times_table(leave[k], T[1, p * depth:(p + 1) * depth], 1)
+                wide_hop(k, p).start()
 
         @pl.when(narrow_out)
         def _():
@@ -154,8 +158,11 @@
     def _():
         @pl.loop(0, chunks)
         def _(k):
-            wide_hop(k).wait_recv()
-            value = times_table(arrive_u[k], T[0], 0) * damp0
+            value = jnp.zeros(leave.shape[1:], F32)
+            for p in range(parts):
+                wide_hop(k, p).wait_recv()
+                value += times_table(arrive_u[p, k], T[0, p * depth:(p + 1) * depth], 0)
+            value = value * damp0
             early_a[k] = value
             leave[k] = times(value, m1.at[0], m1.at[1])
             send(k)
@@ -223,7 +230,8 @@
     def _():
         @pl.loop(0, chunks)
         def _(k):
-            wide_hop(k).wait_send()
+            for p in range(parts):
+                wide_hop(k, p).wait_send()
 
 
 def solution(mesh):
@@ -232,7 +240,7 @@
     def on_device(tab, att, exc):
         segs, heights, half = tab.shape
         modes, sources = exc.shape
-        wide, pieces, chunks = min(4, n - 1), 8, 8
+        wide, pieces, chunks, parts = min(4, n - 1), 8, 8, 2
         rows = sources // cores // chunks
         dma = pltpu.SemaphoreType.DMA
         vmem = pl.BlockSpec(memory_space=pltpu.VMEM)
@@ -250,8 +258,8 @@
                 pltpu.VMEM((2, modes, modes), BF16),
                 pltpu.VMEM((chunks, rows, modes), F32),
                 pltpu.VMEM((chunks, rows, modes), F32),
-                pltpu.VMEM((chunks, rows, heights), F32),
-                pltpu.VMEM((chunks, rows, heights), F32),
+                pltpu.VMEM((parts, chunks, rows, heights // parts), F32),
+                pltpu.VMEM((parts, chunks, rows, heights // parts), F32),
                 pltpu.VMEM((chunks, rows, modes), F32),
                 pltpu.VMEM((cores, chunks, rows, modes), BF16),
                 pltpu.VMEM((sources, modes), BF16),
@@ -260,6 +268,7 @@
                 dma((pieces,)), dma((pieces,)),
                 dma((4,)), dma((4,)),
                 dma((chunks,)), dma((chunks,)),
+                dma((parts, chunks)), dma((parts, chunks)),
                 dma((chunks + 1,)), dma((chunks + 1,)),
             ],
             compiler_params=pltpu.CompilerParams(

time: 88.4 us -> 87.4 us (0.989)
  Pallas kernels: 87.2 us -> 86.3 us
    pallas_call x1, Pallas kernels: 87.2 us -> 86.3 us  [on_device(): pl.pallas_call(functools.partial(kernel, n, wide, pieces, chunks), out_sh...]
where the time goes in v4:
time: 87.4 us; the launch traced here: 87.2 us
  Pallas kernels  86.3 us (99%)
  local copies, waits for them, and re-layouts  0.97 us (1%)
    pallas_call x1, Pallas kernels, on_device(): pl.pallas_call(functools.partial(kernel, n, wide, pieces, chunks), out_sh...  86.3 us

profile of v4, /device:TPU:31, one launch (start us, length us, event | category | flops | bytes accessed | tf_op | source)
XLA Modules:
  0.0 87.2 jit_solution(2326251587191238095)
XLA Ops:
  0.0 86.3 %shard_map.37 = f32[2,1024,128]{2,1,0:T(8,128)S(1)} custom-call(bf16[2,2048,384]{2,1,0:T(8,128)(2,1)} %tab.1, f32[2,768]{1,0:T(2,128)} %att.1, f32[768,128]{1,0:T(8,128)} %exc.1), custom_call_target="tpu_custom_call" | custom-call | tf_op jit(solution)/shard_map/pallas_call | solution.py:247
  86.3 1.0 %copy.5 = f32[2,1024,128]{2,1,0:T(8,128)} copy(f32[2,1024,128]{2,1,0:T(8,128)S(1)} %shard_map.37) | data formatting | bytes 2097152

commit v5 on v4

--- a/solution.py
+++ b/solution.py
@@ -115,6 +115,8 @@
 
     parts = leave_u.shape[0]
     depth = heights // parts
+    wides = leave_u.shape[1]
+    group = chunks // wides
 
     def wide_hop(k, p):
         return remote(leave_u.at[p, k], arrive_u.at[p, k], wd_s.at[p, k], wd_r.at[p, k], ahead)
@@ -123,13 +125,18 @@
         mine = late_r.at[core, k]
         return remote(mine, mine, rd_s.at[k], rd_r.at[k], partner)
 
-    def send(k):
+    def send_group(g):
         @pl.when(wide_out)
         def _():
+            value = leave[pl.ds(g * group, group)].reshape(leave_u.shape[2], modes)
             for p in range(parts):
-                leave_u[p, k] = times_table(leave[k], T[1, p * depth:(p + 1) * depth], 1)
-                wide_hop(k, p).start()
-
+                leave_u[p, g] = times_table(value, T[1, p * depth:(p + 1) * depth], 1)
+                wide_hop(g, p).start()
+
+        for j in range(group):
+            send(g * group + j)
+
+    def send(k):
         @pl.when(narrow_out)
         def _():
             hop(k).start()
@@ -150,22 +157,24 @@
         value = times_table(times_table(start, T[0], 1), T[1], 0) * damp1
         leave[...] = value.reshape(leave.shape)
 
-        @pl.loop(0, chunks)
-        def _(k):
-            send(k)
+        @pl.loop(0, wides)
+        def _(k):
+            send_group(k)
 
     @pl.when(wide_in)
     def _():
-        @pl.loop(0, chunks)
-        def _(k):
-            value = jnp.zeros(leave.shape[1:], F32)
+        @pl.loop(0, wides)
+        def _(k):
+            value = jnp.zeros((leave_u.shape[2], modes), F32)
             for p in range(parts):
                 wide_hop(k, p).wait_recv()
                 value += times_table(arrive_u[p, k], T[0, p * depth:(p + 1) * depth], 0)
             value = value * damp0
-            early_a[k] = value
-            leave[k] = times(value, m1.at[0], m1.at[1])
-            send(k)
+            several = pl.ds(k * group, group)
+            shape = (group,) + leave.shape[1:]
+            leave[several] = times(value, m1.at[0], m1.at[1]).reshape(shape)
+            send_group(k)
+            early_a[several] = value.reshape(shape)
 
     @pl.when(narrow_in)
     def _():
@@ -228,7 +237,7 @@
 
     @pl.when(wide_out)
     def _():
-        @pl.loop(0, chunks)
+        @pl.loop(0, wides)
         def _(k):
             for p in range(parts):
                 wide_hop(k, p).wait_send()
@@ -240,7 +249,7 @@
     def on_device(tab, att, exc):
         segs, heights, half = tab.shape
         modes, sources = exc.shape
-        wide, pieces, chunks, parts = min(4, n - 1), 8, 8, 2
+        wide, pieces, chunks, wides, parts = min(4, n - 1), 8, 8, 4, 4
         rows = sources // cores // chunks
         dma = pltpu.SemaphoreType.DMA
         vmem = pl.BlockSpec(memory_space=pltpu.VMEM)
@@ -258,8 +267,8 @@
                 pltpu.VMEM((2, modes, modes), BF16),
                 pltpu.VMEM((chunks, rows, modes), F32),
                 pltpu.VMEM((chunks, rows, modes), F32),
-                pltpu.VMEM((parts, chunks, rows, heights // parts), F32),
-                pltpu.VMEM((parts, chunks, rows, heights // parts), F32),
+                pltpu.VMEM((parts, wides, rows * chunks // wides, heights // parts), F32),
+                pltpu.VMEM((parts, wides, rows * chunks // wides, heights // parts), F32),
                 pltpu.VMEM((chunks, rows, modes), F32),
                 pltpu.VMEM((cores, chunks, rows, modes), BF16),
                 pltpu.VMEM((sources, modes), BF16),
@@ -268,7 +277,7 @@
                 dma((pieces,)), dma((pieces,)),
                 dma((4,)), dma((4,)),
                 dma((chunks,)), dma((chunks,)),
-                dma((parts, chunks)), dma((parts, chunks)),
+                dma((parts, wides)), dma((parts, wides)),
                 dma((chunks + 1,)), dma((chunks + 1,)),
             ],
             compiler_params=pltpu.CompilerParams(

time: 87.4 us -> 87.3 us (level)
  no operation moved by 1% of the time
where the time goes in v5:
time: 87.3 us; the launch traced here: 87.1 us
  Pallas kernels  86.1 us (99%)
  local copies, waits for them, and re-layouts  0.97 us (1%)
    pallas_call x1, Pallas kernels, on_device(): pl.pallas_call(functools.partial(kernel, n, wide, pieces, chunks), out_sh...  86.1 us

profile of v5, /device:TPU:31, one launch (start us, length us, event | category | flops | bytes accessed | tf_op | source)
XLA Modules:
  0.0 87.1 jit_solution(15111792418372887573)
XLA Ops:
  0.0 86.1 %shard_map.37 = f32[2,1024,128]{2,1,0:T(8,128)S(1)} custom-call(bf16[2,2048,384]{2,1,0:T(8,128)(2,1)} %tab.1, f32[2,768]{1,0:T(2,128)} %att.1, f32[768,128]{1,0:T(8,128)} %exc.1), custom_call_target="tpu_custom_call" | custom-call | tf_op jit(solution)/shard_map/pallas_call | solution.py:256
  86.1 1.0 %copy.5 = f32[2,1024,128]{2,1,0:T(8,128)} copy(f32[2,1024,128]{2,1,0:T(8,128)S(1)} %shard_map.37) | data formatting | bytes 2097152

commit v6 on v5

--- a/solution.py
+++ b/solution.py
@@ -186,17 +186,23 @@
             copy.wait_recv()
             acc[...] += contract(E[rows], T[0, rows], 0, 0)
 
-        scaled = acc[...] * damp0
-        m0[0, own_rows], m0[1, own_rows] = split(scaled)
-        product = times(scaled, m1.at[0], m1.at[1])
-        pr[0, own_rows], pr[1, own_rows] = split(product)
-        mats = [
-            remote(ref.at[k, own_rows], ref.at[k, own_rows], mat_s.at[2 * i + k], mat_r.at[2 * i + k], partner)
-            for i, ref in enumerate((pr, m0)) for k in range(2)
-        ]
-        for c in mats:
-            c.start()
-        for c in mats[:2]:
+        tile = 128
+        tiles = half // tile
+
+        def exchange(ref, rows, i):
+            return remote(ref.at[:, rows], ref.at[:, rows], mat_s.at[i], mat_r.at[i], partner)
+
+        mats = []
+        for t in range(tiles):
+            rows = pl.ds(pl.multiple_of(core * half + t * tile, 128), tile)
+            scaled = acc[t * tile:(t + 1) * tile] * damp0
+            m0[0, rows], m0[1, rows] = split(scaled)
+            pr[0, rows], pr[1, rows] = split(times(scaled, m1.at[0], m1.at[1]))
+            mats.append(exchange(pr, rows, t))
+            mats[t].start()
+        mats.append(exchange(m0, own_rows, tiles))
+        mats[tiles].start()
+        for c in mats[:tiles]:
             c.wait()
 
         @pl.loop(0, chunks)
@@ -205,8 +211,7 @@
             leave[k] = times(arrive[k], pr.at[0], pr.at[1])
             send(k)
 
-        for c in mats[2:]:
-            c.wait()
+        mats[tiles].wait()
         value = times(arrive[...].reshape(count, modes), m0.at[0], m0.at[1])
         early_a[...] = value.reshape(early_a.shape)
 
@@ -275,7 +280,7 @@
                 dma((segs,)),
                 dma((segs,)), dma((segs,)),
                 dma((pieces,)), dma((pieces,)),
-                dma((4,)), dma((4,)),
+                dma((half // 128 + 1,)), dma((half // 128 + 1,)),
                 dma((chunks,)), dma((chunks,)),
                 dma((parts, wides)), dma((parts, wides)),
                 dma((chunks + 1,)), dma((chunks + 1,)),

time: 87.3 us -> 86.8 us (level)
  no operation moved by 1% of the time
where the time goes in v6:
time: 86.8 us; the launch traced here: 86.6 us
  Pallas kernels  85.7 us (99%)
  local copies, waits for them, and re-layouts  0.97 us (1%)
    pallas_call x1, Pallas kernels, on_device(): pl.pallas_call(functools.partial(kernel, n, wide, pieces, chunks), out_sh...  85.7 us

profile of v6, /device:TPU:31, one launch (start us, length us, event | category | flops | bytes accessed | tf_op | source)
XLA Modules:
  0.0 86.6 jit_solution(12812840507914643252)
XLA Ops:
  0.0 85.7 %shard_map.37 = f32[2,1024,128]{2,1,0:T(8,128)S(1)} custom-call(bf16[2,2048,384]{2,1,0:T(8,128)(2,1)} %tab.1, f32[2,768]{1,0:T(2,128)} %att.1, f32[768,128]{1,0:T(8,128)} %exc.1), custom_call_target="tpu_custom_call" | custom-call | tf_op jit(solution)/shard_map/pallas_call | solution.py:261
  85.7 1.0 %copy.5 = f32[2,1024,128]{2,1,0:T(8,128)} copy(f32[2,1024,128]{2,1,0:T(8,128)S(1)} %shard_map.37) | data formatting | bytes 2097152

commit v7 on v6

--- a/solution.py
+++ b/solution.py
@@ -254,7 +254,7 @@
     def on_device(tab, att, exc):
         segs, heights, half = tab.shape
         modes, sources = exc.shape
-        wide, pieces, chunks, wides, parts = min(4, n - 1), 8, 8, 4, 4
+        wide, pieces, chunks, wides, parts = min(5, n - 1), 8, 8, 4, 4
         rows = sources // cores // chunks
         dma = pltpu.SemaphoreType.DMA
         vmem = pl.BlockSpec(memory_space=pltpu.VMEM)

time: 86.8 us -> 87.1 us (level)
  no operation moved by 1% of the time
where the time goes in v7:
time: 87.1 us; the launch traced here: 86.9 us
  Pallas kernels  85.9 us (99%)
  local copies, waits for them, and re-layouts  0.97 us (1%)
    pallas_call x1, Pallas kernels, on_device(): pl.pallas_call(functools.partial(kernel, n, wide, pieces, chunks), out_sh...  85.9 us

profile of v7, /device:TPU:31, one launch (start us, length us, event | category | flops | bytes accessed | tf_op | source)
XLA Modules:
  0.0 86.9 jit_solution(14827919055814704111)
XLA Ops:
  0.0 85.9 %shard_map.37 = f32[2,1024,128]{2,1,0:T(8,128)S(1)} custom-call(bf16[2,2048,384]{2,1,0:T(8,128)(2,1)} %tab.1, f32[2,768]{1,0:T(2,128)} %att.1, f32[768,128]{1,0:T(8,128)} %exc.1), custom_call_target="tpu_custom_call" | custom-call | tf_op jit(solution)/shard_map/pallas_call | solution.py:261
  85.9 1.0 %copy.5 = f32[2,1024,128]{2,1,0:T(8,128)} copy(f32[2,1024,128]{2,1,0:T(8,128)S(1)} %shard_map.37) | data formatting | bytes 2097152
